TPU v7x, 32 devices: a whole 2x2x4 slice. The times are simulated.
32 devices in a mesh: row: 8 (over y, x, core), col: 4 (over z).
Axes of the slice: x: 2, y: 2, z: 4, core: 2. Of those that a mesh axis runs over, the one named last changes fastest.
Arguments:
- matrix: float32 [16, 8, 128, 32, 4, 128], P(None, 'row', None, None, 'col'), may hold values from -6 to 6
- reflectors: float32 [32, 4, 128, 512], P(None, 'col'), as said below
Outputs:
- updated: float32 [16, 8, 128, 32, 4, 128], P(None, 'row', None, None, 'col')
Inputs may be any that keep to these rules, and one draw needn't show every extreme that they name: Read as a 16384 x 512 matrix, the columns of reflectors are orthonormal.
All inputs are finite; a program needn't handle non-finite values.
Results may differ from a plain program's by a relative error of at most 0.0001.
Values sent between devices are 32-bit elements; how exact they have to be, the bound alone decides.
No kernel may reach another device: no remote copies, remote signals or barrier semaphores. Data moves between devices by JAX's collectives and lax.ppermute only.
A program may use at most 192 MiB of HBM per device.

v0:
```python
import jax
import jax.numpy as jnp
from jax import lax
from jax.sharding import PartitionSpec as P


def from_root(value, axis, source):
    kept = jnp.where(lax.axis_index(axis) == source, value, 0).astype(value.dtype)
    return lax.psum(kept, axis)


def per_device(matrix, reflectors):
    row_count = lax.axis_size("row")
    col_count = lax.axis_size("col")
    stride = row_count // col_count
    row_index = lax.axis_index("row")
    col_index = lax.axis_index("col")
    row_tiles, _, tile_size, col_tiles, _, _ = matrix.shape
    total_rank = reflectors.shape[3]
    local_rows = row_tiles * tile_size
    local_cols = col_tiles * tile_size
    current = matrix.reshape(local_rows, local_cols)
    row_ids = (
        (jnp.arange(row_tiles)[:, None] * row_count + row_index) * tile_size
        + jnp.arange(tile_size)[None, :]
    ).reshape(-1)
    col_ids = (
        (jnp.arange(col_tiles)[:, None] * col_count + col_index) * tile_size
        + jnp.arange(tile_size)[None, :]
    ).reshape(-1)
    lower_mask = row_ids[:, None] >= col_ids[None, :]
    strict_mask = row_ids[:, None] > col_ids[None, :]
    refl_cols = reflectors.reshape(local_cols, total_rank)

    def pick_rows(source):
        breadth = source.shape[1]
        blocks = source.reshape(row_tiles, stride, tile_size, breadth)
        chosen = lax.dynamic_index_in_dim(blocks, row_index // col_count, axis=1, keepdims=False)
        return chosen.reshape(local_rows, breadth)

    def matmul(left_side, right_side):
        return jnp.dot(
            left_side,
            right_side,
            precision=lax.Precision.HIGHEST,
            preferred_element_type=jnp.float32,
        )

    def inner(left_side, right_side):
        return lax.dot_general(
            left_side,
            right_side,
            (((0,), (0,)), ((), ())),
            precision=lax.Precision.HIGHEST,
            preferred_element_type=jnp.float32,
        )

    refl_rows = from_root(pick_rows(refl_cols), "col", row_index % col_count)
    direct_part = matmul(jnp.where(lower_mask, current, 0.0), refl_cols)
    trans_part = inner(jnp.where(strict_mask, current, 0.0), refl_rows)
    direct = lax.psum(direct_part, "col")
    transposed = lax.psum(trans_part, "row")
    w_rows = direct + from_root(pick_rows(transposed), "col", row_index % col_count)
    breadth = direct.shape[1]
    pieces = []
    for offset in range(stride):
        moved = from_root(direct, "row", col_index + offset * col_count)
        pieces.append(moved.reshape(row_tiles, tile_size, breadth))
    w_cols = transposed + jnp.stack(pieces, axis=1).reshape(local_cols, breadth)
    projection = lax.psum(inner(refl_rows, w_rows), "row")
    w_rows = w_rows - 0.5 * matmul(refl_rows, projection)
    w_cols = w_cols - 0.5 * matmul(refl_cols, projection)
    left_side = jnp.concatenate([refl_rows, w_rows], axis=1)
    right_side = jnp.concatenate([w_cols, refl_cols], axis=1)
    current = current - lax.dot_general(
        left_side,
        right_side,
        (((1,), (1,)), ((), ())),
        precision=lax.Precision.HIGHEST,
        preferred_element_type=jnp.float32,
    )
    return jnp.where(lower_mask, current, 0.0).reshape(matrix.shape)


def solution(mesh):
    placed = (P(None, "row", None, None, "col", None), P(None, "col", None, None))
    return jax.shard_map(
        per_device,
        mesh=mesh,
        in_specs=placed,
        out_specs=P(None, "row", None, None, "col", None),
        check_vma=False,
    )
```

profile of v0, /device:TPU:0, one launch (start us, length us, event | category | flops | bytes accessed | tf_op | source)
XLA Modules:
  0.0 1057.2 jit_solution(7333891088313638128)
XLA Ops:
  6.5 0.0 all-reduce.7.cloned.1.call-start
  6.5 4.9 bitcast_select_fusion.3
  11.4 0.0 all-reduce.7.cloned.1.call-update
  11.4 0.0 all-reduce.9.cloned.1.call-start
  11.5 0.1 iota_add_fusion.1
  11.6 0.1 iota_add_fusion
  11.7 157.6 %all-reduce.7.cloned.1.call-done = f32[2048,512]{1,0:T(8,128)} async-done(((f32[2048,512]{1,0:T(8,128)}), f32[2048,512]{1,0:T(8,128)}) %all-reduce.7.cloned.1.call-update) | async-done | bytes 4194320 | tf_op jit(solution)/shard_map/psum | solution.py:9
  169.3 67.3 %fusion.4 = f32[4096,512]{1,0:T(8,128)} fusion(f32[2048,512]{1,0:T(8,128)} %all-reduce.7.cloned.1.call-done, f32[256,8,32,128]{3,2,1,0:T(8,128)} %bitcast.60, s32[4096]{0:T(1024)S(1)} %get-tuple-element.16, s32[2048]{0:T(1024)S(1)} %get-tuple-element.14), kind=kOutput, calls=%fused_computation.7 | convolution fusion | flops 51556384768 | bytes 46161920 | tf_op jit(solution)/shard_map/dot_general | solution.py:50
  236.6 0.0 all-reduce.9.cloned.1.call-update
  236.6 0.0 all-reduce.13.cloned.1.call-start
  236.7 114.5 %fusion = f32[16,128,32,128]{3,2,1,0:T(8,128)} fusion(f32[16,1,128,32,1,128]{5,4,3,2,1,0:T(1,128)} %param.2, s32[32,128]{1,0:T(8,128)S(1)} %get-tuple-element.15, s32[16,128]{1,0:T(8,128)S(1)} %get-tuple-element.13), kind=kLoop, calls=%fused_computation.1 | loop fusion | flops 16777216 | bytes 67133440 | tf_op jit(solution)/shard_map/jit(_where)/select_n | solution.py:59
  351.1 64.4 %fusion.1 = f32[2048,512]{1,0:T(8,128)} fusion(f32[4096,512]{1,0:T(8,128)} %bitcast.64, f32[256,8,32,128]{3,2,1,0:T(8,128)} %bitcast.62), kind=kOutput, calls=%fused_computation.2 | convolution fusion | flops 51539607552 | bytes 46137344 | tf_op jit(solution)/shard_map/dot_general | solution.py:42
  415.5 4.9 bitcast_select_fusion.2
  420.4 0.0 all-reduce.13.cloned.1.call-update
  420.4 0.0 all-reduce.11.cloned.1.call-start
  420.5 289.9 %all-reduce.13.cloned.1.call-done = (f32[2048,512]{1,0:T(8,128)}, f32[2048,512]{1,0:T(8,128)}) async-done(((f32[2048,512]{1,0:T(8,128)}, f32[2048,512]{1,0:T(8,128)}), (f32[2048,512]{1,0:T(8,128)}, f32[2048,512]{1,0:T(8,128)})) %all-reduce.13.cloned.1.call-update) | async-done | bytes 8388624 | tf_op jit(solution)/shard_map/psum | solution.py:61
  710.4 9.0 fusion.22
  719.4 2.0 copy-done
  721.4 0.0 copy-done.2
  721.4 7.7 fusion.23
  729.1 0.0 all-reduce.11.cloned.1.call-update
  729.1 136.8 %all-reduce.11.cloned.1.call-done = (f32[16,1,128,512]{3,2,0,1:T(8,128)}, f32[16,1,128,512]{3,2,0,1:T(8,128)}, f32[512,512]{1,0:T(8,128)}) async-done(((f32[16,1,128,512]{3,2,0,1:T(8,128)}, f32[16,1,128,512]{3,2,0,1:T(8,128)}, f32[512,512]{1,0:T(8,128)}), (f32[16,1,128,512]{3,2,0,1:T(8,128)}, f32[16,1,128,512]{3,2,0,1:T(8,128)}, f32[512,512]{1,0:T(8,128)})) %all-reduce.11.cloned.1.call-update) | async-done | bytes 9437200 | tf_op jit(solution)/shard_map/psum | solution.py:9
  865.9 4.5 pad_maximum_fusion
  870.4 0.0 copy-start.1
  870.4 0.0 copy-start.3
  870.4 1.6 copy.5
  872.0 0.6 copy-done.1
  872.6 0.3 copy-done.3
  872.9 10.3 multiply_subtract_fusion
  883.2 18.6 %bitcast_subtract_fusion.1 = f32[4096,512]{1,0:T(8,128)} fusion(f32[4096,512]{1,0:T(8,128)} %all-reduce.9.cloned.1.call-done, f32[16,2,128,512]{3,2,1,0:T(8,128)S(1)} %copy.5, f32[512,512]{1,0:T(8,128)S(1)} %copy-done.3, f32[4096,512]{1,0:T(8,128)} %bitcast.65), kind=kOutput, calls=%fused_computation.22 | convolution fusion | flops 12891193344 | bytes 34603008 | tf_op jit(solution)/shard_map/dot_general | solution.py:42
  901.8 121.1 %fusion.6 = f32[256,8,32,128]{3,1,2,0:T(8,128)} fusion(f32[256,8,32,128]{3,2,1,0:T(8,128)} %bitcast.61, f32[4096,512]{1,0:T(8,128)} %bitcast.66, f32[4096,512]{1,0:T(8,128)} %bitcast_subtract_fusion.1, s32[4096]{0:T(1024)S(1)} %get-tuple-element.16, s32[2048]{0:T(1024)S(1)} %get-tuple-element.14, f32[2048,512]{1,0:T(8,128)} %multiply_subtract_fusion, ...), kind=kOutput, calls=%fused_computation.9 | convolution fusion | flops 103110672384 | bytes 92299264 | tf_op jit(solution)/shard_map/dot_general | solution.py:75
  1022.9 27.6 %copy.11 = f32[256,8,32,128]{3,2,1,0:T(8,128)} copy(f32[256,8,32,128]{3,1,2,0:T(8,128)} %fusion.6) | data formatting | bytes 67108864
  (5 shorter events, 0.0 us)
Async XLA Ops:
  6.5 162.8 %all-reduce.7.cloned.1.call-start = ((), (), s32[]{:S(2)}) async-start(), calls=%async_computation | async-start | bytes 8388608 | tf_op jit(solution)/shard_map/psum | solution.py:9
  11.4 404.1 %all-reduce.9.cloned.1.call-start = ((), (), s32[]{:S(2)}) async-start(), calls=%async_computation.1 | async-start | bytes 16777216 | tf_op jit(solution)/shard_map/psum | solution.py:62
  236.6 473.8 %all-reduce.13.cloned.1.call-start = ((), (), s32[]{:S(2)}) async-start(), calls=%async_computation.3 | async-start | bytes 16777216 | tf_op jit(solution)/shard_map/psum | solution.py:61
  420.4 445.5 %all-reduce.11.cloned.1.call-start = ((), (), s32[]{:S(2)}) async-start(), calls=%async_computation.2 | async-start | bytes 18874368 | tf_op jit(solution)/shard_map/psum | solution.py:9
  710.4 11.0 %copy-start.2 = (f32[2048,512]{1,0:T(8,128)S(1)}, f32[2048,512]{1,0:T(8,128)}, u32[]{:S(2)}) copy-start(f32[2048,512]{1,0:T(8,128)} %all-reduce.7.cloned.1.call-done) | copy-start | bytes 12582916
  719.4 2.0 copy-start
  870.4 2.2 copy-start.1
  870.4 2.5 copy-start.3
Sparse Core Ops, SparseCore 0:
  11.6 157.6 all-reduce.6
  236.7 125.1 all-reduce.8
  420.6 289.8 all-reduce.12
  729.3 136.6 all-reduce.10
where the time goes:
time: 1070 us; the launch traced here: 1060 us
  waiting for transfers between devices  584 us (55%)
  matrix products  289 us (27%)
  other arithmetic  138 us (13%)
  local copies, waits for them, and re-layouts  32 us (3%)
  between operations  13.4 us (1%)
    psum x2, waiting for transfers between devices, from_root(): return lax.psum(kept, axis)  294 us
    psum x1, waiting for transfers between devices, per_device(): direct = lax.psum(direct_part, 'col')  290 us
    dot_general x1, matrix products, per_device(): lax.dot_general(left_side, right_side, (((1,), (1,)), ((), ())), precisio...  121 us
    select_n x1, other arithmetic, per_device(): direct_part = matmul(jnp.where(lower_mask, current, 0.0), refl_cols)  114 us
    dot_general x3, matrix products, matmul(): jnp.dot(left_side, right_side, precision=lax.Precision.HIGHEST, preferred...  93.3 us
    dot_general x2, matrix products, inner(): lax.dot_general(left_side, right_side, (((0,), (0,)), ((), ())), precisio...  75 us
    unnamed x9, local copies, waits for them, and re-layouts  30.4 us
  transfers between devices with their start and end apart: 4, of which 3 were waited for; matrix products, arithmetic and copies ran while one was open for 17% of the time, Pallas kernels for 0%

commit v1 on v0

--- a/solution.py
+++ b/solution.py
@@ -6,7 +6,7 @@
 
 def from_root(value, axis, source):
     kept = jnp.where(lax.axis_index(axis) == source, value, 0).astype(value.dtype)
-    return lax.psum(kept, axis)
+    return jnp.sum(lax.all_gather(kept, axis), axis=0)
 
 
 def per_device(matrix, reflectors):

time: 1070 us -> 1550 us (1.45)
  waiting for transfers between devices: 584 us -> 1020 us
  other arithmetic: 138 us -> 191 us
    all_gather x0 -> x4, waiting for transfers between devices: none -> 694 us  [from_root(): return jnp.sum(lax.all_gather(kept, axis), axis=0)]
    psum x2 -> x1, waiting for transfers between devices: 294 us -> 54.5 us  [per_device(): projection = lax.psum(inner(refl_rows, w_rows), 'row')]
    psum x1, waiting for transfers between devices: 290 us -> 145 us  [per_device(): direct = lax.psum(direct_part, 'col')]
    psum x1, waiting for transfers between devices: 0.01 us -> 124 us  [per_device(): transposed = lax.psum(trans_part, 'row')]
    reduce_sum x0 -> x4, other arithmetic: none -> 53.5 us  [from_root(): return jnp.sum(lax.all_gather(kept, axis), axis=0)]
  transfers between devices with their start and end apart: 4 -> 7, of which waited for: 3 -> 7; matrix products, arithmetic and copies ran while one was open for 17% -> 14% of each run, Pallas kernels for 0% -> 0%
where the time goes in v1:
time: 1550 us; the launch traced here: 1540 us
  waiting for transfers between devices  1020 us (66%)
  matrix products  291 us (19%)
  other arithmetic  191 us (12%)
  local copies, waits for them, and re-layouts  29.6 us (2%)
    all_gather x4, waiting for transfers between devices, from_root(): return jnp.sum(lax.all_gather(kept, axis), axis=0)  694 us
    psum x1, waiting for transfers between devices, per_device(): direct = lax.psum(direct_part, 'col')  145 us
    psum x1, waiting for transfers between devices, per_device(): transposed = lax.psum(trans_part, 'row')  124 us
    dot_general x1, matrix products, per_device(): lax.dot_general(left_side, right_side, (((1,), (1,)), ((), ())), precisio...  121 us
    select_n x1, other arithmetic, per_device(): direct_part = matmul(jnp.where(lower_mask, current, 0.0), refl_cols)  114 us
    dot_general x3, matrix products, matmul(): jnp.dot(left_side, right_side, precision=lax.Precision.HIGHEST, preferred...  94 us
    dot_general x2, matrix products, inner(): lax.dot_general(left_side, right_side, (((0,), (0,)), ((), ())), precisio...  75.6 us
    psum x1, waiting for transfers between devices, per_device(): projection = lax.psum(inner(refl_rows, w_rows), 'row')  54.5 us
  transfers between devices with their start and end apart: 7, of which 7 were waited for; matrix products, arithmetic and copies ran while one was open for 14% of the time, Pallas kernels for 0%

profile of v1, /device:TPU:0, one launch (start us, length us, event | category | flops | bytes accessed | tf_op | source)
XLA Modules:
  0.0 1544.1 jit_solution(9322523840755138310)
XLA Ops:
  6.5 4.9 dynamic-slice_select_fusion.1
  11.4 0.0 all-reduce.6.cloned.1.call-start
  11.5 0.1 iota_add_fusion.1
  11.6 0.1 iota_add_fusion
  11.7 289.4 %all-gather.7.cloned.1.call-done = f32[4,2048,512]{2,1,0:T(8,128)} async-done(((f32[1,2048,512]{2,1,0:T(8,128)}), f32[4,2048,512]{2,1,0:T(8,128)}) %all-gather.7.cloned.1.call-update) | async-done | bytes 16777232 | tf_op jit(solution)/shard_map/all_gather | solution.py:9
  301.1 10.4 reduce_sum.36
  311.4 67.8 %fusion.4 = f32[4096,512]{1,0:T(8,128)} fusion(f32[2048,512]{1,0:T(8,128)} %reduce_sum.36, f32[256,8,32,128]{3,2,1,0:T(8,128)} %bitcast.58, s32[4096]{0:T(1024)S(1)} %get-tuple-element.11, s32[2048]{0:T(1024)S(1)} %get-tuple-element.9), kind=kOutput, calls=%fused_computation.7 | convolution fusion | flops 51556384768 | bytes 46161920 | tf_op jit(solution)/shard_map/dot_general | solution.py:50
  379.3 0.0 all-gather.9.cloned.1.call-start
  379.3 124.5 %all-reduce.6.cloned.1.call-done = f32[4096,512]{1,0:T(8,128)} async-done(((f32[4096,512]{1,0:T(8,128)}), f32[4096,512]{1,0:T(8,128)}) %all-reduce.6.cloned.1.call-update) | async-done | bytes 8388624 | tf_op jit(solution)/shard_map/psum | solution.py:62
  503.8 4.8 dynamic-slice_select_fusion
  508.6 0.0 all-reduce.4.cloned.1.call-start
  508.7 113.6 %fusion = f32[16,128,32,128]{3,2,1,0:T(8,128)} fusion(f32[16,1,128,32,1,128]{5,4,3,2,1,0:T(1,128)} %param.2, s32[32,128]{1,0:T(8,128)S(1)} %get-tuple-element.10, s32[16,128]{1,0:T(8,128)S(1)} %get-tuple-element.8), kind=kLoop, calls=%fused_computation.1 | loop fusion | flops 16777216 | bytes 67133440 | tf_op jit(solution)/shard_map/jit(_where)/select_n | solution.py:59
  622.3 64.3 %fusion.1 = f32[2048,512]{1,0:T(8,128)} fusion(f32[4096,512]{1,0:T(8,128)} %bitcast.64, f32[256,8,32,128]{3,2,1,0:T(8,128)} %bitcast.60), kind=kOutput, calls=%fused_computation.2 | convolution fusion | flops 51539607552 | bytes 46137344 | tf_op jit(solution)/shard_map/dot_general | solution.py:42
  686.7 109.0 %all-gather.9.cloned.1.call-done = f32[4,2048,512]{2,1,0:T(8,128)} async-done(((f32[1,2048,512]{2,1,0:T(8,128)}), f32[4,2048,512]{2,1,0:T(8,128)}) %all-gather.9.cloned.1.call-update) | async-done | bytes 16777232 | tf_op jit(solution)/shard_map/all_gather | solution.py:9
  795.7 10.6 reduce_sum.37
  806.3 144.8 %all-reduce.4.cloned.1.call-done = f32[2048,512]{1,0:T(8,128)} async-done(((f32[2048,512]{1,0:T(8,128)}), f32[2048,512]{1,0:T(8,128)}) %all-reduce.4.cloned.1.call-update) | async-done | bytes 4194320 | tf_op jit(solution)/shard_map/psum | solution.py:61
  951.1 9.0 fusion.22
  960.2 1.9 copy-done.2
  962.1 7.8 fusion.23
  969.9 0.5 all-gather.13.cloned.1.call-update
  970.5 0.4 all-gather.11.cloned.1.call-start
  970.9 0.3 all-gather.11.cloned.1.call-update
  971.2 54.5 %all-reduce.8.cloned.1.call-done = f32[512,512]{1,0:T(8,128)} async-done(((f32[512,512]{1,0:T(8,128)}), f32[512,512]{1,0:T(8,128)}) %all-reduce.8.cloned.1.call-update) | async-done | bytes 1048592 | tf_op jit(solution)/shard_map/psum | solution.py:70
  1025.7 10.8 multiply_subtract_fusion
  1036.6 150.8 %all-gather.13.cloned.1.call-done = f32[16384,512]{1,0:T(8,128)} async-done(((f32[2048,512]{1,0:T(8,128)}), f32[16384,512]{1,0:T(8,128)}) %all-gather.13.cloned.1.call-update) | async-done | bytes 33554448 | tf_op jit(solution)/shard_map/all_gather | solution.py:9
  1187.4 17.5 %reduce_sum.39 = f32[2048,512]{1,0:T(8,128)} reduce(f32[8,2048,512]{2,1,0:T(8,128)} %bitcast.61, f32[]{:T(128)} %constant.56.clone.1), dimensions={0}, to_apply=%region_6.7 | reduce | flops 7340032 | bytes 37748740 | tf_op jit(solution)/shard_map/reduce_sum | solution.py:9
  1204.9 145.1 %all-gather.11.cloned.1.call-done = f32[16384,512]{1,0:T(8,128)} async-done(((f32[2048,512]{1,0:T(8,128)}), f32[16384,512]{1,0:T(8,128)}) %all-gather.11.cloned.1.call-update) | async-done | bytes 33554448 | tf_op jit(solution)/shard_map/all_gather | solution.py:9
  1350.0 15.0 reduce_sum.38
  1365.0 4.6 pad_maximum_fusion
  1369.6 18.8 %bitcast_subtract_fusion.1 = f32[4096,512]{1,0:T(8,128)} fusion(f32[4096,512]{1,0:T(8,128)} %all-reduce.6.cloned.1.call-done, f32[16,2,128,512]{3,2,1,0:T(8,128)S(1)} %pad_maximum_fusion, f32[512,512]{1,0:T(8,128)S(1)} %copy-done.3, f32[4096,512]{1,0:T(8,128)} %bitcast.65), kind=kOutput, calls=%fused_computation.22 | convolution fusion | flops 12891193344 | bytes 34603008 | tf_op jit(solution)/shard_map/dot_general | solution.py:42
  1388.5 121.0 %fusion.6 = f32[256,8,32,128]{3,1,2,0:T(8,128)} fusion(f32[256,8,32,128]{3,2,1,0:T(8,128)} %bitcast.59, f32[4096,512]{1,0:T(8,128)} %bitcast.66, f32[4096,512]{1,0:T(8,128)} %bitcast_subtract_fusion.1, s32[4096]{0:T(1024)S(1)} %get-tuple-element.11, s32[2048]{0:T(1024)S(1)} %get-tuple-element.9, f32[2048,512]{1,0:T(8,128)} %multiply_subtract_fusion, ...), kind=kOutput, calls=%fused_computation.9 | convolution fusion | flops 103110672384 | bytes 92299264 | tf_op jit(solution)/shard_map/dot_general | solution.py:75
  1509.4 27.6 %copy.7 = f32[256,8,32,128]{3,2,1,0:T(8,128)} copy(f32[256,8,32,128]{3,1,2,0:T(8,128)} %fusion.6) | data formatting | bytes 67108864
  (17 shorter events, 0.2 us)
Async XLA Ops:
  6.5 294.5 %all-gather.7.cloned.1.call-start = ((), (), s32[]{:S(2)}) async-start(), calls=%async_computation | async-start | bytes 20971520 | tf_op jit(solution)/shard_map/all_gather | solution.py:9
  11.4 492.4 %all-reduce.6.cloned.1.call-start = ((), (), s32[]{:S(2)}) async-start(), calls=%async_computation.2 | async-start | bytes 16777216 | tf_op jit(solution)/shard_map/psum | solution.py:62
  379.3 416.4 %all-gather.9.cloned.1.call-start = ((), (), s32[]{:S(2)}) async-start(), calls=%async_computation.3 | async-start | bytes 20971520 | tf_op jit(solution)/shard_map/all_gather | solution.py:9
  508.6 442.5 %all-reduce.4.cloned.1.call-start = ((), (), s32[]{:S(2)}) async-start(), calls=%async_computation.1 | async-start | bytes 8388608 | tf_op jit(solution)/shard_map/psum | solution.py:61
  686.6 339.1 %all-reduce.8.cloned.1.call-start = ((), (), s32[]{:S(2)}) async-start(), calls=%async_computation.4 | async-start | bytes 2097152 | tf_op jit(solution)/shard_map/psum | solution.py:70
  951.1 11.0 copy-start
  960.2 2.0 copy-start.2
  969.9 217.5 %all-gather.13.cloned.1.call-start = ((), (), s32[]{:S(2)}) async-start(), calls=%async_computation.6 | async-start | bytes 37748736 | tf_op jit(solution)/shard_map/all_gather | solution.py:9
  970.5 379.5 %all-gather.11.cloned.1.call-start = ((), (), s32[]{:S(2)}) async-start(), calls=%async_computation.5 | async-start | bytes 37748736 | tf_op jit(solution)/shard_map/all_gather | solution.py:9
  1365.0 4.6 copy-start.3
  1369.6 18.8 %copy-start.1 = (f32[2048,512]{1,0:T(8,128)S(1)}, f32[2048,512]{1,0:T(8,128)}, u32[]{:S(2)}) copy-start(f32[2048,512]{1,0:T(8,128)} %reduce_sum.36) | copy-start | bytes 12582916
Sparse Core Ops, SparseCore 0:
  11.6 289.4 all-gather.6
  379.4 124.3 all-reduce.5
  508.8 286.8 all-gather.8
  797.9 153.1 all-reduce.3
  970.0 55.6 all-reduce.7
  1027.5 159.8 all-gather.12
  1189.3 160.6 all-gather.10
